TPU v7x, 128 devices: a whole 4x4x4 slice. The times are simulated.
128 devices in a mesh: req: 16 (over y, z), tp: 8 (over x, core).
Axes of the slice: x: 4, y: 4, z: 4, core: 2. Of those that a mesh axis runs over, the one named last changes fastest.
Arguments:
- short_tokens: bfloat16 [1536, 3072], P('req')
- long_tokens: bfloat16 [8, 3072], replicated
- norm_gain: bfloat16 [3072], replicated, may hold values from 0.5 to 1.5
- w_query: bfloat16 [3072, 3072], P(None, 'tp'), may hold values from -0.109375 to 0.109375
- w_key: bfloat16 [3072, 1024], P(None, 'tp'), may hold values from -0.109375 to 0.109375
- w_value: bfloat16 [3072, 1024], P(None, 'tp'), may hold values from -0.109375 to 0.109375
- w_out: bfloat16 [3072, 3072], P('tp'), may hold values from -0.109375 to 0.109375
- short_lengths: int32 [1536], P('req'), may hold values from 0 to 127
- long_lengths: int32 [8], replicated, may hold values from 6144 to 8191
- short_cache: bfloat16 [1536, 8, 128, 256], P('req', 'tp'), may hold values from -120 to 120
- long_cache: bfloat16 [8, 8, 8192, 256], P(None, 'tp', 'req'), may hold values from -120 to 120
Outputs:
- short_hidden: bfloat16 [1536, 3072], P('req')
- long_hidden: bfloat16 [8, 3072], replicated
- short_cache_new: bfloat16 [1536, 8, 128, 256], P('req', 'tp')
- long_cache_new: bfloat16 [8, 8, 8192, 256], P(None, 'tp', 'req')
All inputs are finite; a program needn't handle non-finite values.
Results may differ from a plain program's by a relative error of at most 0.0095.
Values may be sent and summed in bfloat16 or wider, within the bound.
A program may use at most 128 MiB of HBM per device.

v0:
```python
import jax
import jax.numpy as jnp
from jax import lax
from jax.sharding import PartitionSpec as P

rope_theta = 500000.0
floor_score = -1e30


def merged(value, axis, join):
    pieces = jax.tree.map(lambda part: lax.all_gather(part, axis), value)
    head = jax.tree.map(lambda part: part[0], pieces)
    tail = jax.tree.map(lambda part: part[1:], pieces)
    total, _ = lax.scan(lambda total, slab: (join(total, slab), None), head, tail)
    return total


def rotate(values, positions):
    half = values.shape[-1] // 2
    freq = rope_theta ** (-(jnp.arange(half, dtype=jnp.float32) * 2.0 / values.shape[-1]))
    angle = positions.astype(jnp.float32)[:, None] * freq[None, :]
    cosine = jnp.cos(angle)[:, None, :]
    sine = jnp.sin(angle)[:, None, :]
    front = values[..., :half]
    back = values[..., half:]
    return jnp.concatenate([front * cosine - back * sine, back * cosine + front * sine], axis=-1)


def join_partials(earlier, later):
    peak_one, total_one, summed_one = earlier
    peak_two, total_two, summed_two = later
    peak_new = jnp.maximum(peak_one, peak_two)
    factor_one = jnp.exp(peak_one - peak_new)
    factor_two = jnp.exp(peak_two - peak_new)
    total_new = total_one * factor_one + total_two * factor_two
    summed_new = summed_one * factor_one[..., None] + summed_two * factor_two[..., None]
    return (peak_new, total_new, summed_new)


def per_device(
    short_tokens,
    long_tokens,
    norm_gain,
    w_query,
    w_key,
    w_value,
    w_out,
    short_lengths,
    long_lengths,
    short_cache,
    long_cache,
):
    head_size = short_cache.shape[-1] // 2
    kv_local = short_cache.shape[1]
    short_count = short_tokens.shape[0]
    long_count = long_tokens.shape[0]
    all_tokens = jnp.concatenate([short_tokens, long_tokens], axis=0)
    positions = jnp.concatenate([short_lengths, long_lengths], axis=0)
    total_rows = all_tokens.shape[0]
    residual = all_tokens.astype(jnp.float32)
    normed = (
        residual
        * lax.rsqrt(jnp.mean(residual * residual, axis=-1, keepdims=True) + 1e-05)
        * norm_gain.astype(jnp.float32)
    ).astype(jnp.bfloat16)
    query = jnp.dot(normed, w_query, preferred_element_type=jnp.float32).reshape(
        total_rows, -1, head_size
    )
    group_size = query.shape[1] // kv_local
    query = (
        rotate(query, positions)
        .astype(jnp.bfloat16)
        .reshape(total_rows, kv_local, group_size, head_size)
    )
    key_new = jnp.dot(normed, w_key, preferred_element_type=jnp.float32).reshape(
        total_rows, kv_local, head_size
    )
    key_new = rotate(key_new, positions).astype(jnp.bfloat16)
    value_new = (
        jnp.dot(normed, w_value, preferred_element_type=jnp.float32)
        .reshape(total_rows, kv_local, head_size)
        .astype(jnp.bfloat16)
    )
    fresh = jnp.concatenate([key_new, value_new], axis=-1)
    score_scale = 1.0 / jnp.sqrt(jnp.float32(head_size))
    short_slots = jnp.arange(short_cache.shape[2], dtype=jnp.int32)
    short_write = short_slots[None, :] == short_lengths[:, None]
    short_out = jnp.where(
        short_write[:, None, :, None], fresh[:short_count, :, None, :], short_cache
    )
    short_scores = (
        jnp.einsum(
            "rkgd,rksd->rkgs",
            query[:short_count],
            short_out[..., :head_size],
            preferred_element_type=jnp.float32,
        )
        * score_scale
    )
    short_valid = (short_slots[None, :] <= short_lengths[:, None])[:, None, None, :]
    short_scores = jnp.where(short_valid, short_scores, floor_score)
    short_top = jnp.max(short_scores, axis=-1, keepdims=True)
    short_expo = jnp.where(short_valid, jnp.exp(short_scores - short_top), 0.0)
    short_weights = (short_expo / jnp.sum(short_expo, axis=-1, keepdims=True)).astype(jnp.bfloat16)
    short_mix = jnp.einsum(
        "rkgs,rksd->rkgd",
        short_weights,
        short_out[..., head_size:],
        preferred_element_type=jnp.float32,
    )
    span = long_cache.shape[2]
    first_slot = lax.axis_index("req") * span
    long_slots = first_slot + jnp.arange(span, dtype=jnp.int32)
    long_write = long_slots[None, :] == long_lengths[:, None]
    long_out = jnp.where(long_write[:, None, :, None], fresh[short_count:, :, None, :], long_cache)
    long_scores = (
        jnp.einsum(
            "lkgd,lksd->lkgs",
            query[short_count:],
            long_out[..., :head_size],
            preferred_element_type=jnp.float32,
        )
        * score_scale
    )
    long_valid = (long_slots[None, :] <= long_lengths[:, None])[:, None, None, :]
    long_scores = jnp.where(long_valid, long_scores, floor_score)
    long_peak = jnp.max(long_scores, axis=-1)
    long_expo = jnp.where(long_valid, jnp.exp(long_scores - long_peak[..., None]), 0.0)
    long_total = jnp.sum(long_expo, axis=-1)
    long_summed = jnp.einsum(
        "lkgs,lksd->lkgd",
        long_expo,
        long_out[..., head_size:].astype(jnp.float32),
        precision=lax.Precision.HIGHEST,
    )
    peak_all, total_all, summed_all = merged(
        (long_peak, long_total, long_summed), "req", join_partials
    )
    long_mix = summed_all / total_all[..., None]
    mixed = jnp.concatenate(
        [short_mix.reshape(short_count, -1), long_mix.reshape(long_count, -1)], axis=0
    ).astype(jnp.bfloat16)
    head_terms = jnp.dot(mixed, w_out, preferred_element_type=jnp.float32)
    summed_heads = lax.psum(head_terms, "tp")
    hidden = (residual + summed_heads).astype(jnp.bfloat16)
    return (hidden[:short_count], hidden[short_count:], short_out, long_out)


def solution(mesh):
    placed = (
        P("req", None),
        P(),
        P(),
        P(None, "tp"),
        P(None, "tp"),
        P(None, "tp"),
        P("tp", None),
        P("req"),
        P(),
        P("req", "tp", None, None),
        P(None, "tp", "req", None),
    )
    return jax.shard_map(
        per_device,
        mesh=mesh,
        in_specs=placed,
        out_specs=(P("req", None), P(), P("req", "tp", None, None), P(None, "tp", "req", None)),
        check_vma=False,
    )
```

profile of v0, /device:TPU:1, one launch (start us, length us, event | category | flops | bytes accessed | tf_op | source)
XLA Modules:
  0.0 177.1 jit_solution(13294808918669247572)
XLA Ops:
  7.3 0.8 convert_element_type.43
  8.1 1.4 fusion.7
  9.5 0.7 iota_compare_fusion.1
  10.3 0.8 add_convert_fusion.1
  11.0 0.9 multiply_cosine_fusion.1
  11.9 1.9 %convolution_bitcast_fusion = f32[104,1,128]{2,0,1:T(8,128)S(1)} fusion(bf16[3072,128]{1,0:T(8,128)(2,1)} %param.17, f32[3072]{0:T(1024)S(1)} %convert_element_type.43, f32[104]{0:T(128)S(1)} %add_rsqrt_fusion, bf16[8,3072]{1,0:T(8,128)(2,1)} %param.14, bf16[96,3072]{1,0:T(8,128)(2,1)} %param.13), kind=kOutput, calls=%fused_computation.33 | convolution fusion | flops 84025344 | bytes 1491360 | tf_op jit(solution)/shard_map/dot_general | solution.py:75
  13.8 0.3 fusion.30
  14.1 0.4 fusion.18
  14.5 0.7 pad_maximum_fusion.2
  15.3 1.1 fusion.43
  16.5 0.1 copy.64
  16.6 0.1 copy.65
  16.7 0.7 broadcast_compare_fusion.1
  17.5 1.9 %bitcast_select_fusion.1 = bf16[8,1,512,256]{3,2,0,1:T(8,128)(2,1)S(1)} fusion(bf16[8,1,512,256]{3,2,1,0:T(8,128)(2,1)} %param.23, pred[8,512]{1,0:T(8,128)(4,1)S(1)} %get-tuple-element.102, bf16[8,256]{1,0:T(8,128)(2,1)S(1)} %maximum_bitcast_fusion), kind=kLoop, calls=%fused_computation.17 | loop fusion | flops 1048576 | bytes 4202496 | tf_op jit(solution)/shard_map/jit(_where)/select_n | solution.py:115
  19.4 0.1 subtract_convert_fusion
  19.6 0.5 fusion.47
  20.1 0.6 fusion.19
  20.7 20.7 %all-gather.2 = f32[128,3,128]{2,0,1:T(8,128)S(1)} all-gather(f32[8,3,128]{2,0,1:T(8,128)S(1)} %copy.51), channel_id=4, replica_groups=mesh['req'=16,'tp'=8] {'req'}, dimensions={0}, use_global_device_ids=true | all-gather | bytes 208896 | tf_op jit(solution)/shard_map/all_gather | solution.py:11
  41.4 0.2 fusion.33
  41.6 0.1 copy.50
  41.7 17.6 %all-gather.4 = f32[16,8,3]{1,2,0:T(4,128)S(1)} all-gather(f32[1,8,3]{1,2,0:T(4,128)S(1)} %bitcast.102), channel_id=3, replica_groups=mesh['req'=16,'tp'=8] {'req'}, dimensions={0}, use_global_device_ids=true | all-gather | bytes 1632 | tf_op jit(solution)/shard_map/all_gather | solution.py:11
  59.3 0.1 copy.49
  59.4 16.1 %all-gather.3 = f32[16,8,3]{1,2,0:T(4,128)S(1)} all-gather(f32[1,8,3]{1,2,0:T(4,128)S(1)} %bitcast.103), channel_id=2, replica_groups=mesh['req'=16,'tp'=8] {'req'}, dimensions={0}, use_global_device_ids=true | all-gather | bytes 1632 | tf_op jit(solution)/shard_map/all_gather | solution.py:11
  75.5 6.2 %bitcast_select_fusion = bf16[96,1,128,256]{3,2,0,1:T(8,128)(2,1)S(1)} fusion(bf16[96,1,128,256]{3,2,1,0:T(8,128)(2,1)} %param.22, pred[96,128]{1,0:T(8,128)(4,1)S(1)} %get-tuple-element.106, bf16[96,256]{1,0:T(8,128)(2,1)S(1)} %slice_bitcast_fusion.15), kind=kLoop, calls=%fused_computation.12 | loop fusion | flops 3145728 | bytes 12644352 | tf_op jit(solution)/shard_map/jit(_where)/select_n | solution.py:88
  81.8 1.8 fusion.15
  83.5 0.3 fusion.48
  83.8 1.0 fusion.16
  84.9 4.6 %while.14 = (s32[]{:T(128)}, f32[8,1,3]{0,1,2:T(1,128)S(1)}, f32[8,1,3]{0,1,2:T(1,128)S(1)}, f32[8,1,3,128]{3,2,1,0:T(4,128)S(1)}, f32[15,8,1,3]{1,0,3,2:T(8,128...) while((s32[]{:T(128)}, f32[8,1,3]{0,1,2:T(1,128)S(1)}, ...), condition=%wide.region_6.7_spmd, body=%wide.region_5.6_spmd.sunk | while | flops 9362 | bytes 62877 | solution.py:14
  85.0 0.1 copy.85
  85.1 0.1 fusion.59
  85.3 0.1 copy.85
  85.4 0.1 fusion.59
  85.8 0.1 fusion.59
  85.9 0.1 copy.85
  86.1 0.1 fusion.59
  86.2 0.1 copy.85
  86.4 0.1 fusion.59
  86.5 0.1 copy.85
  86.7 0.1 fusion.59
  86.8 0.1 copy.85
  87.0 0.1 fusion.59
  87.1 0.1 copy.85
  87.3 0.1 fusion.59
  87.4 0.1 copy.85
  87.6 0.1 fusion.59
  87.7 0.1 copy.85
  87.9 0.1 fusion.59
  88.0 0.1 copy.85
  88.2 0.1 fusion.59
  88.3 0.1 copy.85
  88.5 0.1 fusion.59
  88.7 0.1 copy.85
  88.8 0.1 fusion.59
  89.0 0.1 copy.85
  89.1 0.1 fusion.59
  89.3 0.1 copy.85
  89.4 0.1 fusion.59
  89.6 1.6 fusion.21
  91.2 2.9 %fusion.54 = bf16[8,1,512,256]{3,2,1,0:T(8,128)(2,1)} fusion(bf16[8,1,512,256]{3,2,1,0:T(8,128)(2,1)} %param.23, bf16[8,256]{1,0:T(8,128)(2,1)S(1)} %maximum_bitcast_fusion, pred[8,512]{1,0:T(8,128)(4,1)S(1)} %get-tuple-element.102), kind=kLoop, calls=%fused_computation.92 | loop fusion | flops 1048576 | bytes 4202496
  94.1 7.6 %fusion.55 = bf16[96,1,128,256]{3,2,1,0:T(8,128)(2,1)} fusion(bf16[96,1,128,256]{3,2,1,0:T(8,128)(2,1)} %param.22, bf16[96,256]{1,0:T(8,128)(2,1)S(1)} %slice_bitcast_fusion.15, pred[96,128]{1,0:T(8,128)(4,1)S(1)} %get-tuple-element.106), kind=kLoop, calls=%fused_computation.93 | loop fusion | flops 3145728 | bytes 12644352
  101.7 65.6 %all-reduce.2.cloned.1.call-done = f32[104,3072]{1,0:T(8,128)} async-done(((f32[104,3072]{1,0:T(8,128)}), f32[104,3072]{1,0:T(8,128)}) %all-reduce.2.cloned.1.call-update) | async-done | bytes 1277968 | tf_op jit(solution)/shard_map/psum | solution.py:144
  167.3 1.4 fusion.10
  168.7 0.9 slice.107
  169.6 0.6 slice.108
  (99 shorter events, 2.2 us)
Async XLA Ops:
  7.2 82.5 %copy-start = (bf16[384,3072]{1,0:T(8,128)(2,1)S(1)}, bf16[384,3072]{1,0:T(8,128)(2,1)}, u32[]{:S(2)}) copy-start(bf16[384,3072]{1,0:T(8,128)(2,1)} %param.19) | copy-start | bytes 7077892
  7.2 6.9 %copy-start.1 = (bf16[96,3072]{1,0:T(8,128)(2,1)S(1)}, bf16[96,3072]{1,0:T(8,128)(2,1)}, u32[]{:S(2)}) copy-start(bf16[96,3072]{1,0:T(8,128)(2,1)} %param.13) | copy-start | bytes 1769476
  7.2 6.9 %copy-start.4 = (bf16[8,3072]{1,0:T(8,128)(2,1)S(1)}, bf16[8,3072]{1,0:T(8,128)(2,1)}, u32[]{:S(2)}) copy-start(bf16[8,3072]{1,0:T(8,128)(2,1)} %param.14) | copy-start | bytes 147460
  7.2 160.1 %all-reduce.2.cloned.1.call-start = ((), (), s32[]{:S(2)}) async-start(), calls=%async_computation | async-start | bytes 2555904 | tf_op jit(solution)/shard_map/psum | solution.py:144
  7.2 6.9 %copy-start.13 = (bf16[3072,128]{1,0:T(8,128)(2,1)S(1)}, bf16[3072,128]{1,0:T(8,128)(2,1)}, u32[]{:S(2)}) copy-start(bf16[3072,128]{1,0:T(8,128)(2,1)} %param.18) | copy-start | bytes 2359300
  11.9 3.4 %copy-start.12 = (bf16[3072,384]{1,0:T(8,128)(2,1)S(1)}, bf16[3072,384]{1,0:T(8,128)(2,1)}, u32[]{:S(2)}) copy-start(bf16[3072,384]{1,0:T(8,128)(2,1)} %param.16) | copy-start | bytes 7077892
  17.5 2.0 %copy-start.2 = (f32[104,64]{1,0:T(8,128)S(1)}, f32[104,64]{1,0:T(8,128)}, u32[]{:S(2)}) copy-start(f32[104,64]{1,0:T(8,128)} %get-tuple-element.104) | copy-start | bytes 79876
  19.6 21.9 %copy-start.8 = (bf16[104,3,64]{2,1,0:T(4,128)(2,1)}, bf16[104,3,64]{2,1,0:T(4,128)(2,1)S(1)}, u32[]{:S(2)}) copy-start(bf16[104,3,64]{2,1,0:T(4,128)(2,1)S(1)} %get-tuple-element.95) | copy-start | bytes 119812
  19.6 21.8 %copy-start.10 = (bf16[104,3,64]{2,1,0:T(4,128)(2,1)}, bf16[104,3,64]{2,1,0:T(4,128)(2,1)S(1)}, u32[]{:S(2)}) copy-start(bf16[104,3,64]{2,1,0:T(4,128)(2,1)S(1)} %get-tuple-element.96) | copy-start | bytes 119812
  19.6 55.9 %copy-start.3 = (bf16[104,1,256]{2,0,1:T(8,128)(2,1)S(1)}, bf16[104,1,256]{2,0,1:T(8,128)(2,1)}, u32[]{:S(2)}) copy-start(bf16[104,1,256]{2,0,1:T(8,128)(2,1)} %pad_maximum_fusion.2) | copy-start | bytes 159748
  59.3 22.4 %copy-start.6 = (f32[16,8,3]{1,2,0:T(4,128)}, f32[16,8,3]{1,2,0:T(4,128)S(1)}, u32[]{:S(2)}) copy-start(f32[16,8,3]{1,2,0:T(4,128)S(1)} %all-gather.4) | copy-start | bytes 4612
  75.5 6.3 %copy-start.7 = (f32[16,8,3]{1,2,0:T(4,128)}, f32[16,8,3]{1,2,0:T(4,128)S(1)}, u32[]{:S(2)}) copy-start(f32[16,8,3]{1,2,0:T(4,128)S(1)} %all-gather.3) | copy-start | bytes 4612
  75.5 6.2 %copy-start.9 = (bf16[104,3,64]{2,1,0:T(4,128)(2,1)S(1)}, bf16[104,3,64]{2,1,0:T(4,128)(2,1)}, u32[]{:S(2)}) copy-start(bf16[104,3,64]{2,1,0:T(4,128)(2,1)} %copy-done.8) | copy-start | bytes 119812
  75.5 6.2 %copy-start.11 = (bf16[104,3,64]{2,1,0:T(4,128)(2,1)S(1)}, bf16[104,3,64]{2,1,0:T(4,128)(2,1)}, u32[]{:S(2)}) copy-start(bf16[104,3,64]{2,1,0:T(4,128)(2,1)} %copy-done.10) | copy-start | bytes 119812
  83.8 1.1 slice-start
  83.8 1.1 slice-start.1
  94.1 73.2 %copy-start.5 = (bf16[8,3072]{1,0:T(8,128)(2,1)S(1)}, bf16[8,3072]{1,0:T(8,128)(2,1)}, u32[]{:S(2)}) copy-start(bf16[8,3072]{1,0:T(8,128)(2,1)} %param.14) | copy-start | bytes 147460
Sparse Core Ops, SparseCore 0:
  91.3 75.8 all-reduce.1
where the time goes:
time: 179 us; the launch traced here: 177 us
  waiting for transfers between devices  65.6 us (37%)
  blocking collectives  54.4 us (30%)
  other arithmetic  29 us (16%)
  between operations  14.5 us (8%)
  matrix products  8.79 us (5%)
  local copies, waits for them, and re-layouts  4.56 us (3%)
    psum x1, waiting for transfers between devices, per_device(): summed_heads = lax.psum(head_terms, 'tp')  65.6 us
    all_gather x3, blocking collectives, merged(): pieces = jax.tree.map(lambda part: lax.all_gather(part, axis), value)  54.4 us
    unnamed x2, other arithmetic  10.5 us
    select_n x1, other arithmetic, per_device(): jnp.where(short_write[:, None, :, None], fresh[:short_count, :, None, :],...  6.17 us
  transfers between devices with their start and end apart: 1, of which 1 were waited for; matrix products, arithmetic and copies ran while one was open for 6% of the time, Pallas kernels for 0%

commit v1 on v0

v1 whole, which is shorter than its diff:
```python
import functools
import math

import jax
import jax.numpy as jnp
import numpy as np
from jax import lax
from jax.experimental import pallas as pl
from jax.experimental.pallas import tpu as pltpu
from jax.sharding import PartitionSpec as P

rope_theta = 500000.0
floor_score = -1e30
group_rows = 16
MESH = pl.DeviceIdType.MESH
F32 = jnp.float32
BF16 = jnp.bfloat16


def nt_dot(a, b):
    return lax.dot_general(a, b, (((1,), (1,)), ((), ())), preferred_element_type=F32)


def attend_kernel(
    short_len,
    long_len,
    tokens,
    long_tokens,
    gain,
    freq,
    w_query,
    w_key,
    w_value,
    short_cache,
    long_cache,
    att_out,
    part_out,
    short_new,
    long_new,
    tok_v,
    ltok_v,
    normed,
    wq_v,
    wk_v,
    wv_v,
    pos_v,
    q_v,
    qlong_v,
    fresh_v,
    cache_v,
    long_v,
    tok_sem,
    w_sem,
    in_sem,
    out_sem,
    lin_sem,
    lout_sem,
):
    short_count = tokens.shape[0]
    long_count = long_tokens.shape[0]
    slots = short_cache.shape[1]
    span = long_cache.shape[1]
    head = short_cache.shape[2] // 2
    heads = w_query.shape[1] // head
    groups = short_count // group_rows
    rows = heads * group_rows
    lrows = heads * long_count
    scale = 1.0 / math.sqrt(head)

    def cache_in(g):
        view = pl.ds(g * group_rows, group_rows)
        return pltpu.make_async_copy(short_cache.at[view], cache_v.at[view], in_sem.at[g])

    def cache_out(g):
        view = pl.ds(g * group_rows, group_rows)
        return pltpu.make_async_copy(cache_v.at[view], short_new.at[view], out_sem.at[g])

    first = [
        pltpu.make_async_copy(tokens, tok_v, tok_sem.at[0]),
        pltpu.make_async_copy(long_tokens, ltok_v, tok_sem.at[1]),
    ]
    weights = [
        pltpu.make_async_copy(w_key, wk_v, w_sem.at[0]),
        pltpu.make_async_copy(w_value, wv_v, w_sem.at[1]),
        pltpu.make_async_copy(w_query, wq_v, w_sem.at[2]),
    ]
    long_in = pltpu.make_async_copy(long_cache, long_v, lin_sem)
    long_out = pltpu.make_async_copy(long_v, long_new, lout_sem)
    for copy in first + weights:
        copy.start()
    long_in.start()
    for g in range(groups):
        cache_in(g).start()

    sub8 = lax.broadcasted_iota(jnp.int32, (8, head), 0)
    for tile in range((short_count + long_count) // 8):
        value = jnp.zeros((8, head), jnp.int32)
        for j in range(8):
            r = tile * 8 + j
            length = short_len[r] if r < short_count else long_len[r - short_count]
            value = jnp.where(sub8 == j, length, value)
        pos_v[tile * 8 : tile * 8 + 8, :] = value

    gain_row = gain[...].astype(F32)

    def norm_rows(value):
        value = value.astype(F32)
        mean = jnp.mean(value * value, axis=-1, keepdims=True)
        return (value * lax.rsqrt(mean + 1e-05) * gain_row).astype(BF16)

    for copy in first:
        copy.wait()

    def norm_step(i, carry):
        view = pl.ds(pl.multiple_of(i * 16, 16), 16)
        normed[view, :] = norm_rows(tok_v[view, :])
        return carry

    lax.fori_loop(0, short_count // 16, norm_step, 0)
    tail = jnp.concatenate([ltok_v[...].astype(F32), jnp.zeros((16 - long_count, tok_v.shape[1]), F32)], axis=0)
    normed[short_count : short_count + 16, :] = norm_rows(tail)

    total_rows = short_count + long_count
    angle = pos_v[...].astype(F32) * freq[...]
    cosine = jnp.cos(angle)
    lane = lax.broadcasted_iota(jnp.int32, angle.shape, 1)
    sine = jnp.where(lane < head // 2, -jnp.sin(angle), jnp.sin(angle))

    def rotate(value):
        return value * cosine + pltpu.roll(value, head // 2, 1) * sine

    weights[0].wait()
    key = jnp.dot(normed[...], wk_v[...], preferred_element_type=F32)[:total_rows]
    fresh_v[:, :head] = rotate(key).astype(BF16).astype(F32)
    weights[1].wait()
    value = jnp.dot(normed[...], wv_v[...], preferred_element_type=F32)[:total_rows]
    fresh_v[:, head:] = value.astype(BF16).astype(F32)
    weights[2].wait()
    query = jnp.dot(normed[...], wq_v[...], preferred_element_type=F32)[:total_rows]
    for h in range(heads):
        rotated = rotate(query[:, h * head : (h + 1) * head])
        q_v[:, h * head : (h + 1) * head] = rotated[:short_count].astype(BF16)
        qlong_v[h * long_count : (h + 1) * long_count, :] = rotated[short_count:]

    sub16 = lax.broadcasted_iota(jnp.int32, (16, 2 * head), 0)

    def patch(ref, slot, limit, row):
        start = pl.multiple_of(lax.clamp(0, slot // 16, limit // 16 - 1) * 16, 16)
        old = ref[pl.ds(start, 16), :].astype(F32)
        new = fresh_v[pl.ds(row, 1), :]
        ref[pl.ds(start, 16), :] = jnp.where(sub16 + start == slot, new, old).astype(BF16)

    first_slot = lax.axis_index("req") * span
    long_in.wait()
    for l in range(long_count):
        patch(long_v.at[l], long_len[l] - first_slot, span, short_count + l)
    qlong = qlong_v[...].astype(BF16)
    row_of = lax.rem(lax.broadcasted_iota(jnp.int32, (lrows, span), 0), long_count)
    slot_of = lax.broadcasted_iota(jnp.int32, (lrows, span), 1) + first_slot
    long_pos = jnp.concatenate([pos_v[short_count:total_rows, :]] * heads, axis=0)
    long_pos = jnp.concatenate([long_pos] * (span // head), axis=1)
    long_valid = slot_of <= long_pos
    scores = jnp.full((lrows, span), floor_score, F32)
    for l in range(long_count):
        piece = nt_dot(qlong, long_v[l, :, :head])
        scores = jnp.where(row_of == l, piece, scores)
    scores = jnp.where(long_valid, scores * scale, floor_score)
    peak = jnp.max(scores, axis=-1, keepdims=True)
    expo = jnp.where(long_valid, jnp.exp(scores - peak), 0.0)
    total = jnp.sum(expo, axis=-1, keepdims=True)
    summed = jnp.zeros((lrows, head), F32)
    for l in range(long_count):
        weight = jnp.where(row_of == l, expo, 0.0).astype(BF16)
        summed = summed + jnp.dot(weight, long_v[l, :, head:], preferred_element_type=F32)
    part_out[:lrows, :] = summed
    here = lax.broadcasted_iota(jnp.int32, (lrows, head), 0) == lax.broadcasted_iota(
        jnp.int32, (lrows, head), 1
    )
    peak_row = jnp.sum(jnp.where(here, peak, 0.0), axis=0, keepdims=True)
    total_row = jnp.sum(jnp.where(here, total, 0.0), axis=0, keepdims=True)
    part_out[lrows : lrows + 8, :] = jnp.where(sub8 == 0, peak_row, total_row)
    long_out.start()

    row16 = lax.rem(lax.broadcasted_iota(jnp.int32, (rows, head), 0), group_rows)
    lane16 = lax.broadcasted_iota(jnp.int32, (rows, head), 1)

    def group(g, carry):
        cache_in(g).wait()
        base = pl.multiple_of(g * group_rows, group_rows)
        for j in range(group_rows):
            patch(cache_v.at[base + j], short_len[base + j], slots, base + j)
        block = q_v[pl.ds(base, group_rows), :]
        stacked = jnp.concatenate([block[:, h * head : (h + 1) * head] for h in range(heads)], axis=0)
        score = jnp.full((rows, slots), floor_score, F32)
        for j in range(group_rows):
            piece = nt_dot(stacked, cache_v[base + j, :, :head])
            score = jnp.where(row16 == j, piece, score)
        valid = lane16 <= jnp.concatenate([pos_v[pl.ds(base, group_rows), :]] * heads, axis=0)
        score = jnp.where(valid, score * scale, floor_score)
        top = jnp.max(score, axis=-1, keepdims=True)
        expo_s = jnp.where(valid, jnp.exp(score - top), 0.0)
        weight = expo_s / jnp.sum(expo_s, axis=-1, keepdims=True)
        mix = jnp.zeros((rows, head), F32)
        for j in range(0, group_rows, 2):
            pair = jnp.concatenate(
                [jnp.where(row16 == i, weight, 0.0).astype(BF16) for i in (j, j + 1)], axis=1
            )
            values = cache_v[pl.ds(base + j, 2), :, head:].reshape(2 * slots, head)
            mix = mix + jnp.dot(pair, values, preferred_element_type=F32)
        att_out[pl.ds(base, group_rows), :] = jnp.concatenate(
            [mix[h * group_rows : (h + 1) * group_rows] for h in range(heads)], axis=1
        ).astype(BF16)
        cache_out(g).start()
        return carry

    lax.fori_loop(0, groups, group, 0)
    for g in range(groups):
        cache_out(g).wait()
    long_out.wait()


def merge_parts(parts, lrows, head):
    here = lax.broadcasted_iota(jnp.int32, (lrows, head), 0) == lax.broadcasted_iota(
        jnp.int32, (lrows, head), 1
    )
    peaks = [part[lrows : lrows + 1, :] for part in parts]
    totals = [part[lrows + 1 : lrows + 2, :] for part in parts]
    top = functools.reduce(jnp.maximum, peaks)
    total = jnp.zeros_like(top)
    summed = jnp.zeros((lrows, head), F32)
    for part, peak, some in zip(parts, peaks, totals):
        factor = jnp.exp(peak - top)
        total = total + some * factor
        column = jnp.sum(jnp.where(here, factor, 0.0), axis=1, keepdims=True)
        summed = summed + part[:lrows, :] * column
    return top, total, summed


def project_kernel(
    tp_size,
    grid_size,
    att,
    part,
    w_out,
    tokens,
    long_tokens,
    hidden,
    long_hidden,
    w_v,
    res_v,
    lres_v,
    part_y,
    part_z,
    mine_v,
    pair_send,
    pair_recv,
    own_v,
    chip_send,
    chip_recv,
    hid_v,
    lsend_v,
    lrecv_v,
    lhid_v,
    w_sem,
    res_sem,
    y_send,
    y_recv,
    z_send,
    z_recv,
    ps_sem,
    pr_sem,
    cs_sem,
    cr_sem,
    gs_sem,
    gr_sem,
    fs_sem,
    fr_sem,
    ls_sem,
    lr_sem,
    lgs_sem,
    lgr_sem,
    out_sem,
    lout_sem,
):
    req = lax.axis_index("req")
    me = lax.axis_index("tp")
    chips = tp_size // 2
    core = lax.rem(me, 2)
    chip = me // 2
    row = req // grid_size
    col = lax.rem(req, grid_size)
    lrows = part.shape[0] - 8
    head = part.shape[1]
    long_count = long_tokens.shape[0]
    heads = lrows // long_count
    width = w_out.shape[1] // tp_size

    def at_tp(index):
        return (req, index)

    partner = chip * 2 + 1 - core
    peers = [lax.rem(me + d, tp_size) for d in range(1, tp_size)]
    row_peers = [(lax.rem(row + d, grid_size) * grid_size + col, me) for d in range(1, grid_size)]
    col_peers = [(row * grid_size + lax.rem(col + d, grid_size), me) for d in range(1, grid_size)]
    chip_peers = [lax.rem(chip + d, chips) for d in range(chips)]

    barrier = pltpu.get_barrier_semaphore()
    everyone = [at_tp(index) for index in peers] + row_peers + col_peers
    for device in everyone:
        pl.semaphore_signal(barrier, inc=1, device_id=device, device_id_type=MESH)

    def columns(j):
        return pl.ds(pl.multiple_of(j * width, width), width)

    w_copies = []
    for j in range(tp_size):
        w_copies.append(pltpu.make_async_copy(w_out.at[:, columns(j)], w_v.at[j], w_sem.at[j]))
        w_copies[-1].start()
    res_copy = pltpu.make_async_copy(tokens.at[:, columns(me)], res_v, res_sem.at[0])
    lres_copy = pltpu.make_async_copy(long_tokens.at[:, columns(me)], lres_v, res_sem.at[1])
    res_copy.start()
    lres_copy.start()
    pl.semaphore_wait(barrier, len(everyone))

    def remote(src, dst, send, recv, device):
        return pltpu.make_async_remote_copy(
            src_ref=src, dst_ref=dst, send_sem=send, recv_sem=recv, device_id=device, device_id_type=MESH
        )

    y_copies = [
        remote(part, part_y.at[d], y_send.at[d], y_recv.at[d], device) for d, device in enumerate(row_peers)
    ]
    for copy in y_copies:
        copy.start()
    for copy in w_copies:
        copy.wait()

    order = [chips // 2] + [d for d in range(1, chips) if d != chips // 2] + [0]
    pair_copies = []
    for d in order:
        j = chip_peers[d] * 2 + 1 - core
        pair_send[d] = jnp.dot(att[...], w_v[j], preferred_element_type=F32).astype(BF16)
        copy = remote(pair_send.at[d], pair_recv.at[d], ps_sem.at[d], pr_sem.at[d], at_tp(partner))
        copy.start()
        pair_copies.append(copy)
    for d in range(chips):
        j = chip_peers[d] * 2 + core
        own_v[d] = jnp.dot(att[...], w_v[j], preferred_element_type=F32)
    chip_copies = []
    for place, d in enumerate(order):
        pair_copies[place].wait_recv()
        summed = own_v[d] + pair_recv[d].astype(F32)
        if d == 0:
            own_v[d] = summed
        else:
            chip_send[d - 1] = summed.astype(BF16)
            copy = remote(
                chip_send.at[d - 1],
                chip_recv.at[d - 1],
                cs_sem.at[d - 1],
                cr_sem.at[d - 1],
                at_tp(chip_peers[d] * 2 + core),
            )
            copy.start()
            chip_copies.append(copy)

    sub8 = lax.broadcasted_iota(jnp.int32, (8, head), 0)
    for copy in y_copies:
        copy.wait_recv()
    top, total, summed = merge_parts([part[...]] + [part_y[d] for d in range(grid_size - 1)], lrows, head)
    mine_v[:lrows, :] = summed
    mine_v[lrows:, :] = jnp.where(sub8 == 0, top, total)
    z_copies = [
        remote(mine_v, part_z.at[d], z_send.at[d], z_recv.at[d], device) for d, device in enumerate(col_peers)
    ]
    for copy in z_copies:
        copy.start()
    for copy in z_copies:
        copy.wait_recv()
    top, total, summed = merge_parts([mine_v[...]] + [part_z[d] for d in range(grid_size - 1)], lrows, head)
    here = lax.broadcasted_iota(jnp.int32, (lrows, head), 0) == lax.broadcasted_iota(
        jnp.int32, (lrows, head), 1
    )
    mixed = summed / jnp.sum(jnp.where(here, total, 0.0), axis=1, keepdims=True)
    long_att = jnp.concatenate(
        [mixed[h * long_count : (h + 1) * long_count] for h in range(heads)], axis=1
    ).astype(BF16)
    long_copies = []
    for d in range(tp_size):
        j = lax.rem(me + d, tp_size)
        lsend_v[d] = jnp.dot(long_att, w_v[j], preferred_element_type=F32)
        if d:
            copy = remote(
                lsend_v.at[d], lrecv_v.at[d - 1], ls_sem.at[d - 1], lr_sem.at[d - 1], at_tp(peers[d - 1])
            )
            copy.start()
            long_copies.append(copy)

    res_copy.wait()
    lres_copy.wait()
    acc = own_v[0] + res_v[...].astype(F32)
    for d in range(1, chips):
        chip_copies[order.index(d)].wait_recv()
        acc = acc + chip_recv[d - 1].astype(F32)
    hid_v[me] = acc.astype(BF16)
    gather = []
    for d in range(1, chips):
        copy = remote(
            hid_v.at[me], hid_v.at[me], gs_sem.at[d - 1], gr_sem.at[d - 1], at_tp(chip_peers[d] * 2 + core)
        )
        copy.start()
        gather.append(copy)
    forward = [remote(hid_v.at[me], hid_v.at[me], fs_sem.at[0], fr_sem.at[0], at_tp(partner))]
    forward[0].start()
    outs = []

    def put(j):
        copy = pltpu.make_async_copy(hid_v.at[j], hidden.at[:, columns(j)], out_sem.at[len(outs)])
        copy.start()
        outs.append(copy)

    put(me)

    for copy in long_copies:
        copy.wait_recv()
    lacc = lsend_v[0] + lres_v[...].astype(F32)
    for d in range(tp_size - 1):
        lacc = lacc + lrecv_v[d]
    lhid_v[me] = lacc.astype(BF16)
    long_gather = []
    for d in range(tp_size - 1):
        copy = remote(lhid_v.at[me], lhid_v.at[me], lgs_sem.at[d], lgr_sem.at[d], at_tp(peers[d]))
        copy.start()
        long_gather.append(copy)

    for d in range(1, chips):
        source = lax.rem(chip + chips - d, chips) * 2 + core
        gather[d - 1].wait_recv()
        copy = remote(hid_v.at[source], hid_v.at[source], fs_sem.at[d], fr_sem.at[d], at_tp(partner))
        copy.start()
        forward.append(copy)
        put(source)
    for d in range(chips):
        forward[d].wait_recv()
        put(lax.rem(chip + chips - d, chips) * 2 + 1 - core)
    for copy in long_gather:
        copy.wait_recv()
    louts = []
    for j in range(tp_size):
        copy = pltpu.make_async_copy(lhid_v.at[j], long_hidden.at[:, columns(j)], lout_sem.at[j])
        copy.start()
        louts.append(copy)
    for copy in y_copies + pair_copies + chip_copies + z_copies + long_copies + gather + forward + long_gather:
        copy.wait_send()
    for copy in outs + louts:
        copy.wait()


def per_device(
    tp_size,
    req_size,
    short_tokens,
    long_tokens,
    norm_gain,
    w_query,
    w_key,
    w_value,
    w_out,
    short_lengths,
    long_lengths,
    short_cache,
    long_cache,
):
    short_count, model = short_tokens.shape
    long_count = long_tokens.shape[0]
    slots, head = short_cache.shape[2], short_cache.shape[3] // 2
    span = long_cache.shape[2]
    query_width = w_query.shape[1]
    heads = query_width // head
    total_rows = short_count + long_count
    lrows = heads * long_count
    groups = short_count // group_rows
    half = rope_theta ** (-(np.arange(head // 2, dtype=np.float64) * 2.0 / head))
    freq = np.concatenate([half, half]).astype(np.float32)[None, :]
    short_in = short_cache.reshape(short_count, slots, 2 * head)
    long_in = long_cache.reshape(long_count, span, 2 * head)
    hbm = pl.BlockSpec(memory_space=pl.ANY)
    vmem = pl.BlockSpec(memory_space=pltpu.VMEM)
    smem = pl.BlockSpec(memory_space=pltpu.SMEM)
    dma = pltpu.SemaphoreType.DMA
    att, part, short_new, long_new = pl.pallas_call(
        attend_kernel,
        name="attend",
        out_shape=(
            jax.ShapeDtypeStruct((short_count, query_width), BF16),
            jax.ShapeDtypeStruct((lrows + 8, head), F32),
            jax.ShapeDtypeStruct(short_in.shape, BF16),
            jax.ShapeDtypeStruct(long_in.shape, BF16),
        ),
        in_specs=[smem, smem, hbm, hbm, vmem, vmem, hbm, hbm, hbm, hbm, hbm],
        out_specs=(vmem, vmem, hbm, hbm),
        scratch_shapes=[
            pltpu.VMEM((short_count, model), BF16),
            pltpu.VMEM((long_count, model), BF16),
            pltpu.VMEM((short_count + 16, model), BF16),
            pltpu.VMEM(w_query.shape, BF16),
            pltpu.VMEM(w_key.shape, BF16),
            pltpu.VMEM(w_value.shape, BF16),
            pltpu.VMEM((total_rows, head), jnp.int32),
            pltpu.VMEM((short_count, query_width), BF16),
            pltpu.VMEM((lrows, head), F32),
            pltpu.VMEM((total_rows, 2 * head), F32),
            pltpu.VMEM(short_in.shape, BF16),
            pltpu.VMEM(long_in.shape, BF16),
            dma((2,)),
            dma((3,)),
            dma((groups,)),
            dma((groups,)),
            dma,
            dma,
        ],
        compiler_params=pltpu.CompilerParams(vmem_limit_bytes=40 * 1024 * 1024),
    )(
        short_lengths,
        long_lengths,
        short_tokens,
        long_tokens,
        norm_gain.reshape(1, model),
        freq,
        w_query,
        w_key,
        w_value,
        short_in,
        long_in,
    )

    chips = tp_size // 2
    grid_size = int(math.isqrt(req_size))
    width = model // tp_size
    hidden, long_hidden = pl.pallas_call(
        functools.partial(project_kernel, tp_size, grid_size),
        name="project",
        out_shape=(
            jax.ShapeDtypeStruct((short_count, model), BF16),
            jax.ShapeDtypeStruct((long_count, model), BF16),
        ),
        in_specs=[vmem, vmem, hbm, hbm, hbm],
        out_specs=(hbm, hbm),
        scratch_shapes=[
            pltpu.VMEM((tp_size, query_width, width), BF16),
            pltpu.VMEM((short_count, width), BF16),
            pltpu.VMEM((long_count, width), BF16),
            pltpu.VMEM((grid_size - 1, lrows + 8, head), F32),
            pltpu.VMEM((grid_size - 1, lrows + 8, head), F32),
            pltpu.VMEM((lrows + 8, head), F32),
            pltpu.VMEM((chips, short_count, width), BF16),
            pltpu.VMEM((chips, short_count, width), BF16),
            pltpu.VMEM((chips, short_count, width), F32),
            pltpu.VMEM((chips - 1, short_count, width), BF16),
            pltpu.VMEM((chips - 1, short_count, width), BF16),
            pltpu.VMEM((tp_size, short_count, width), BF16),
            pltpu.VMEM((tp_size, long_count, width), F32),
            pltpu.VMEM((tp_size - 1, long_count, width), F32),
            pltpu.VMEM((tp_size, long_count, width), BF16),
            dma((tp_size,)),
            dma((2,)),
            dma((grid_size - 1,)),
            dma((grid_size - 1,)),
            dma((grid_size - 1,)),
            dma((grid_size - 1,)),
            dma((chips,)),
            dma((chips,)),
            dma((chips - 1,)),
            dma((chips - 1,)),
            dma((chips - 1,)),
            dma((chips - 1,)),
            dma((chips,)),
            dma((chips,)),
            dma((tp_size - 1,)),
            dma((tp_size - 1,)),
            dma((tp_size - 1,)),
            dma((tp_size - 1,)),
            dma((tp_size,)),
            dma((tp_size,)),
        ],
        compiler_params=pltpu.CompilerParams(
            vmem_limit_bytes=24 * 1024 * 1024, collective_id=0, has_side_effects=True
        ),
    )(att, part, w_out, short_tokens, long_tokens)
    return hidden, long_hidden, short_new.reshape(short_cache.shape), long_new.reshape(long_cache.shape)


def solution(mesh):
    placed = (
        P("req", None),
        P(),
        P(),
        P(None, "tp"),
        P(None, "tp"),
        P(None, "tp"),
        P("tp", None),
        P("req"),
        P(),
        P("req", "tp", None, None),
        P(None, "tp", "req", None),
    )
    return jax.shard_map(
        functools.partial(per_device, mesh.shape["tp"], mesh.shape["req"]),
        mesh=mesh,
        in_specs=placed,
        out_specs=(P("req", None), P(), P("req", "tp", None, None), P(None, "tp", "req", None)),
        check_vma=False,
    )
```

time: 179 us -> 50.5 us (0.28)
  waiting for transfers between devices: 65.6 us -> 0 us
  blocking collectives: 54.4 us -> 0 us
  Pallas kernels: 0 us -> 35.1 us
  other arithmetic: 29 us -> 0 us
  between operations: 14.5 us -> 0.67 us
  local copies, waits for them, and re-layouts: 4.56 us -> 14.3 us
  matrix products: 8.79 us -> 0 us
    psum x1 -> x0, waiting for transfers between devices: 65.6 us -> none  [per_device(): summed_heads = lax.psum(head_terms, 'tp')]
    all_gather x3 -> x0, blocking collectives: 54.4 us -> none  [merged(): pieces = jax.tree.map(lambda part: lax.all_gather(part, axis), value)]
    pallas_call x0 -> x2, Pallas kernels: none -> 35.1 us  [the longest x1 24.4 us: per_device(): pl.pallas_call(functools.partial(project_kernel, tp_size, grid_size), nam...]
    unnamed x32 -> x24, local copies, waits for them, and re-layouts: 0.36 us -> 13.6 us
    unnamed x2 -> x0, other arithmetic: 10.5 us -> none
    dot_general x8 -> x0, matrix products: 8.79 us -> none  [the longest x1 1.87 us: per_device(): jnp.dot(normed, w_key, preferred_element_type=jnp.float32)]
    select_n x2 -> x0, other arithmetic: 8.12 us -> none  [the longest x1 6.17 us: per_device(): jnp.where(short_write[:, None, :, None], fresh[:short_count, :, None, :],...]
    convert_element_type x3 -> x0, other arithmetic: 3.02 us -> none  [the longest x1 1.42 us: per_device(): hidden = (residual + summed_heads).astype(jnp.bfloat16)]
  transfers between devices with their start and end apart: 1 -> 0, of which waited for: 1 -> 0; matrix products, arithmetic and copies ran while one was open for 6% -> 0% of each run, Pallas kernels for 0% -> 0%
where the time goes in v1:
time: 50.5 us; the launch traced here: 50 us
  Pallas kernels  35.1 us (70%)
  local copies, waits for them, and re-layouts  14.3 us (28%)
  between operations  0.67 us (1%)
    pallas_call x1, Pallas kernels, per_device(): pl.pallas_call(functools.partial(project_kernel, tp_size, grid_size), nam...  24.4 us
    unnamed x24, local copies, waits for them, and re-layouts  13.6 us
    pallas_call x1, Pallas kernels, per_device(): pl.pallas_call(attend_kernel, name='attend', out_shape=(jax.ShapeDtypeStr...  10.7 us

profile of v1, /device:TPU:1, one launch (start us, length us, event | category | flops | bytes accessed | tf_op | source)
XLA Modules:
  0.0 50.0 jit_solution(5601156853051092113)
XLA Ops:
  0.6 0.7 %reshape.23.gain = bf16[1,3072]{1,0:T(2,128)(2,1)S(1)} reshape(bf16[3072]{0:T(1024)(128)(2,1)} %param.14) | data formatting | bytes 12288 | tf_op jit(solution)/shard_map/reshape | solution.py:528
  1.3 0.0 copy-start
  1.3 2.8 %copy-done = bf16[96,1,128,256]{3,2,1,0:T(8,128)(2,1)S(1)} copy-done((bf16[96,1,128,256]{3,2,1,0:T(8,128)(2,1)S(1)}, bf16[96,1,128,256]{3,2,1,0:T(8,128)(2,1)}, u32[]{:S(2)}) %copy-start) | copy-done | bytes 6291480
  4.1 0.0 copy-start.1
  4.1 1.1 %copy-done.1 = bf16[96,3072]{1,0:T(8,128)(2,1)S(1)} copy-done((bf16[96,3072]{1,0:T(8,128)(2,1)S(1)}, bf16[96,3072]{1,0:T(8,128)(2,1)}, u32[]{:S(2)}) %copy-start.1) | copy-done | bytes 589848
  5.2 0.0 copy-start.3
  5.2 1.7 %copy-done.3 = bf16[3072,384]{1,0:T(8,128)(2,1)S(1)} copy-done((bf16[3072,384]{1,0:T(8,128)(2,1)S(1)}, bf16[3072,384]{1,0:T(8,128)(2,1)}, u32[]{:S(2)}) %copy-start.3) | copy-done | bytes 2359320
  6.8 0.0 copy-start.4
  6.8 1.6 %copy-done.4 = bf16[8,1,512,256]{3,2,1,0:T(8,128)(2,1)S(1)} copy-done((bf16[8,1,512,256]{3,2,1,0:T(8,128)(2,1)S(1)}, bf16[8,1,512,256]{3,2,1,0:T(8,128)(2,1)}, u32[]{:S(2)}) %copy-start.4) | copy-done | bytes 2097176
  8.4 0.0 copy-start.5
  8.4 1.1 %copy-done.5 = bf16[3072,128]{1,0:T(8,128)(2,1)S(1)} copy-done((bf16[3072,128]{1,0:T(8,128)(2,1)S(1)}, bf16[3072,128]{1,0:T(8,128)(2,1)}, u32[]{:S(2)}) %copy-start.5) | copy-done | bytes 786456
  9.6 0.0 copy-start.6
  9.6 1.1 %copy-done.6 = bf16[3072,128]{1,0:T(8,128)(2,1)S(1)} copy-done((bf16[3072,128]{1,0:T(8,128)(2,1)S(1)}, bf16[3072,128]{1,0:T(8,128)(2,1)}, u32[]{:S(2)}) %copy-start.6) | copy-done | bytes 786456
  10.7 0.0 copy-start.7
  10.7 0.8 %copy-done.7 = bf16[8,3072]{1,0:T(8,128)(2,1)S(1)} copy-done((bf16[8,3072]{1,0:T(8,128)(2,1)S(1)}, bf16[8,3072]{1,0:T(8,128)(2,1)}, u32[]{:S(2)}) %copy-start.7) | copy-done | bytes 49176
  11.5 0.0 copy-start.8
  11.5 0.7 %copy-done.8 = s32[96]{0:T(128)S(1)} copy-done((s32[96]{0:T(128)S(1)}, s32[96]{0:T(128)}, u32[]{:S(2)}) %copy-start.8) | copy-done | bytes 408
  12.2 0.0 copy-start.9
  12.2 0.7 %copy-done.9 = s32[8]{0:T(128)S(1)} copy-done((s32[8]{0:T(128)S(1)}, s32[8]{0:T(128)}, u32[]{:S(2)}) %copy-start.9) | copy-done | bytes 56
  12.8 0.0 copy-start.10
  12.8 0.7 %copy-done.10 = f32[1,128]{1,0:T(1,128)S(1)} copy-done((f32[1,128]{1,0:T(1,128)S(1)}, f32[1,128]{1,0:T(1,128)}, u32[]{:S(2)}) %copy-start.10) | copy-done | bytes 536
  13.5 0.0 copy-start.2
  13.5 10.7 %attend.1 = (bf16[96,384]{1,0:T(8,128)(2,1)S(1)}, f32[32,128]{1,0:T(8,128)S(1)}, bf16[96,128,256]{2,1,0:T(8,128)(2,1)}, bf16[8,512,256]{2,1,0:T(8,128)(2,1)}) custom-call(s32[96]{0:T(128)S(1)} %copy-done.8, s32[8]{0:T(128)S(1)} %copy-done.9, bf16[96,3072]{1,0:T(8,128)(2,1)S(1)} %copy-done.1, bf16[8,3072]{1,0:T(8,128)(2,1)S(1)} %copy-done.7, ...), custom_call_target="tpu_custom_call" | custom-call | tf_op jit(solution)/shard_map/attend/pallas_call | solution.py:491
  24.1 0.0 copy-done.2
  24.2 24.4 %project.1 = (bf16[96,3072]{1,0:T(8,128)(2,1)S(1)}, bf16[8,3072]{1,0:T(8,128)(2,1)S(1)}) custom-call(bf16[96,384]{1,0:T(8,128)(2,1)S(1)} %get-tuple-element.10.att, f32[32,128]{1,0:T(8,128)S(1)} %get-tuple-element.11.part, bf16[384,3072]{1,0:T(8,128)(2,1)S(1)} %copy-done.2, bf16[96,3072]{1,0:T(8,128)(2,1)S(1)} %copy-done.1, bf16[8,3072]{1,0:T(8,128)(2,1)S(1)} %copy-done.7), custom_call_target="tpu_custom_call" | custom-call | tf_op jit(solution)/shard_map/project/pallas_call | solution.py:540
  48.6 0.8 %copy.20 = bf16[96,3072]{1,0:T(8,128)(2,1)} copy(bf16[96,3072]{1,0:T(8,128)(2,1)S(1)} %get-tuple-element.24) | data formatting | bytes 1179648
  49.4 0.6 %copy.21 = bf16[8,3072]{1,0:T(8,128)(2,1)} copy(bf16[8,3072]{1,0:T(8,128)(2,1)S(1)} %get-tuple-element.25) | data formatting | bytes 98304
Async XLA Ops:
  1.3 2.8 %copy-start = (bf16[96,1,128,256]{3,2,1,0:T(8,128)(2,1)S(1)}, bf16[96,1,128,256]{3,2,1,0:T(8,128)(2,1)}, u32[]{:S(2)}) copy-start(bf16[96,1,128,256]{3,2,1,0:T(8,128)(2,1)} %param.21) | copy-start | bytes 18874372
  4.1 1.1 %copy-start.1 = (bf16[96,3072]{1,0:T(8,128)(2,1)S(1)}, bf16[96,3072]{1,0:T(8,128)(2,1)}, u32[]{:S(2)}) copy-start(bf16[96,3072]{1,0:T(8,128)(2,1)} %tokens.3) | copy-start | bytes 1769476
  5.2 1.7 %copy-start.3 = (bf16[3072,384]{1,0:T(8,128)(2,1)S(1)}, bf16[3072,384]{1,0:T(8,128)(2,1)}, u32[]{:S(2)}) copy-start(bf16[3072,384]{1,0:T(8,128)(2,1)} %w_query.1) | copy-start | bytes 7077892
  6.8 1.6 %copy-start.4 = (bf16[8,1,512,256]{3,2,1,0:T(8,128)(2,1)S(1)}, bf16[8,1,512,256]{3,2,1,0:T(8,128)(2,1)}, u32[]{:S(2)}) copy-start(bf16[8,1,512,256]{3,2,1,0:T(8,128)(2,1)} %param.22) | copy-start | bytes 6291460
  8.4 1.1 %copy-start.5 = (bf16[3072,128]{1,0:T(8,128)(2,1)S(1)}, bf16[3072,128]{1,0:T(8,128)(2,1)}, u32[]{:S(2)}) copy-start(bf16[3072,128]{1,0:T(8,128)(2,1)} %w_key.1) | copy-start | bytes 2359300
  9.6 1.1 %copy-start.6 = (bf16[3072,128]{1,0:T(8,128)(2,1)S(1)}, bf16[3072,128]{1,0:T(8,128)(2,1)}, u32[]{:S(2)}) copy-start(bf16[3072,128]{1,0:T(8,128)(2,1)} %w_value.1) | copy-start | bytes 2359300
  10.7 0.8 %copy-start.7 = (bf16[8,3072]{1,0:T(8,128)(2,1)S(1)}, bf16[8,3072]{1,0:T(8,128)(2,1)}, u32[]{:S(2)}) copy-start(bf16[8,3072]{1,0:T(8,128)(2,1)} %long_tokens.3) | copy-start | bytes 147460
  11.5 0.7 %copy-start.8 = (s32[96]{0:T(128)S(1)}, s32[96]{0:T(128)}, u32[]{:S(2)}) copy-start(s32[96]{0:T(128)} %short_len.1) | copy-start | bytes 1156
  12.2 0.7 %copy-start.9 = (s32[8]{0:T(128)S(1)}, s32[8]{0:T(128)}, u32[]{:S(2)}) copy-start(s32[8]{0:T(128)} %long_len.1) | copy-start | bytes 100
  12.8 0.7 %copy-start.10 = (f32[1,128]{1,0:T(1,128)S(1)}, f32[1,128]{1,0:T(1,128)}, u32[]{:S(2)}) copy-start(f32[1,128]{1,0:T(1,128)} %constant.2.clone.freq) | copy-start | bytes 1540
  13.5 10.7 %copy-start.2 = (bf16[384,3072]{1,0:T(8,128)(2,1)S(1)}, bf16[384,3072]{1,0:T(8,128)(2,1)}, u32[]{:S(2)}) copy-start(bf16[384,3072]{1,0:T(8,128)(2,1)} %w_out.1) | copy-start | bytes 7077892
